TPU v7x, 32 devices: a whole 2x2x4 slice. The times are simulated.
32 devices in a mesh: dx: 4 (over y, core), dy: 4 (over z), band: 2 (over x).
Axes of the slice: x: 2, y: 2, z: 4, core: 2. Of those that a mesh axis runs over, the one named last changes fastest.
Arguments:
- states: float32 [24, 32, 8, 512], P('dx', 'dy', None, 'band'), may hold values from -6 to 6
- potential: float32 [24, 32, 8], P('dx', 'dy'), may hold values from -1 to 1
Outputs:
- orthonormal: float32 [24, 32, 8, 512], P('dx', 'dy', None, 'band')
All inputs are finite; a program needn't handle non-finite values.
Results may differ from a plain program's by a relative error of at most 0.000073.
Values sent between devices are 32-bit elements; how exact they have to be, the bound alone decides.
No kernel may reach another device: no remote copies, remote signals or barrier semaphores. Data moves between devices by JAX's collectives and lax.ppermute only.
A program may use at most 64 MiB of HBM per device.

v0:
```python
import jax
import jax.numpy as jnp
from jax import lax
from jax.sharding import PartitionSpec as P

DEGREE = 3
coeffs = (
    -5369.0 / 1800.0,
    12.0 / 7.0,
    -15.0 / 56.0,
    10.0 / 189.0,
    -1.0 / 112.0,
    2.0 / 1925.0,
    -1.0 / 16632.0,
)
half_width = 5.0
centre_value = 7.0


def with_halo(cells, sides, width):
    for axis, dim in sides:
        count = lax.axis_size(axis)
        head = lax.slice_in_dim(cells, 0, width, axis=dim)
        tail = lax.slice_in_dim(cells, cells.shape[dim] - width, cells.shape[dim], axis=dim)
        cells = jnp.concatenate(
            [
                lax.ppermute(tail, axis, [(i, (i + 1) % count) for i in range(count)]),
                cells,
                lax.ppermute(head, axis, [((i + 1) % count, i) for i in range(count)]),
            ],
            axis=dim,
        )
    return cells


def apply_ham(field, potential):
    padded = with_halo(field, (("dx", 0), ("dy", 1)), 6)
    size_x = field.shape[0]
    size_y = field.shape[1]
    lap = 3.0 * coeffs[0] * field
    for shift in range(1, 7):
        near = (
            padded[6 + shift : 6 + shift + size_x, 6 : 6 + size_y]
            + padded[6 - shift : 6 - shift + size_x, 6 : 6 + size_y]
        )
        near = (
            near
            + padded[6 : 6 + size_x, 6 + shift : 6 + shift + size_y]
            + padded[6 : 6 + size_x, 6 - shift : 6 - shift + size_y]
        )
        near = near + jnp.roll(field, shift, 2) + jnp.roll(field, -shift, 2)
        lap = lap + coeffs[shift] * near
    return -0.5 * lap + potential[..., None] * field


def shards(states, potential):
    prev = states
    cur = (apply_ham(states, potential) - centre_value * states) / half_width
    for step in range(1, DEGREE):
        nxt = 2.0 * (apply_ham(cur, potential) - centre_value * cur) / half_width - prev
        prev, cur = (cur, nxt)
    block = cur.shape[3]
    cells = cur.shape[0] * cur.shape[1] * cur.shape[2]
    local = cur.reshape(cells, block)
    gathered = lax.all_gather(local, "band", axis=1, tiled=True)
    total = cells * lax.axis_size("dx") * lax.axis_size("dy")
    partial_gram = (
        jnp.dot(
            gathered.T,
            gathered,
            precision=lax.Precision.HIGHEST,
            preferred_element_type=jnp.float32,
        )
        / total
    )
    correlation = lax.psum(partial_gram, ("dx", "dy"))
    factor = jnp.linalg.cholesky(correlation)
    eye = jnp.eye(correlation.shape[0], dtype=jnp.float32)
    inverse = jax.scipy.linalg.solve_triangular(factor, eye, lower=True)
    my_rows = lax.dynamic_slice_in_dim(inverse, lax.axis_index("band") * block, block, 0)
    result = jnp.dot(
        gathered, my_rows.T, precision=lax.Precision.HIGHEST, preferred_element_type=jnp.float32
    )
    return result.reshape(cur.shape)


def solution(mesh):
    return jax.shard_map(
        shards,
        mesh=mesh,
        in_specs=(P("dx", "dy", None, "band"), P("dx", "dy", None)),
        out_specs=P("dx", "dy", None, "band"),
        check_vma=False,
    )
```

profile of v0, /device:TPU:0, one launch (start us, length us, event | category | flops | bytes accessed | tf_op | source)
XLA Modules:
  0.0 442.6 jit_solution(4787194779673460491)
XLA Ops:
  7.0 1.9 collective-permute-start
  13.8 2.6 collective-permute-done.1
  16.6 2.2 collective-permute-done
  19.1 3.7 collective-permute-start.2
  23.0 19.9 %collective-permute-done.2 = f32[18,6,8,256]{3,2,1,0:T(8,128)S(1)} collective-permute-done((f32[18,6,8,256]{3,2,1,0:T(8,128)S(1)}, f32[18,6,8,256]{3,2,1,0:T(8,128)S(1)}, u32[]{:S(2)}, u32[]{:S(2)}) %collective-permute-start.2) | collective-permute-done | bytes 884768 | tf_op jit(solution)/shard_map/ppermute | solution.py:29
  42.8 19.5 %collective-permute-done.3 = f32[18,6,8,256]{3,2,1,0:T(8,128)S(1)} collective-permute-done((f32[18,6,8,256]{3,2,1,0:T(8,128)S(1)}, f32[18,6,8,256]{3,2,1,0:T(8,128)S(1)}, u32[]{:S(2)}, u32[]{:S(2)}) %collective-permute-start.3) | collective-permute-done | bytes 884768 | tf_op jit(solution)/shard_map/ppermute | solution.py:27
  62.3 1.9 broadcast_multiply_fusion
  65.2 9.0 %collective-permute-done.4 = f32[6,8,8,256]{3,2,1,0:T(8,128)S(1)} collective-permute-done((f32[6,8,8,256]{3,2,1,0:T(8,128)S(1)}, f32[6,8,8,256]{3,2,1,0:T(8,128)S(1)}, u32[]{:S(2)}, u32[]{:S(2)}) %collective-permute-start.4) | collective-permute-done | bytes 393248 | tf_op jit(solution)/shard_map/ppermute | solution.py:29
  78.5 19.5 %collective-permute-done.6 = f32[18,6,8,256]{3,2,1,0:T(8,128)S(1)} collective-permute-done((f32[18,6,8,256]{3,2,1,0:T(8,128)S(1)}, f32[18,6,8,256]{3,2,1,0:T(8,128)S(1)}, u32[]{:S(2)}, u32[]{:S(2)}) %collective-permute-start.6) | collective-permute-done | bytes 884768 | tf_op jit(solution)/shard_map/ppermute | solution.py:29
  98.0 18.8 %collective-permute-done.7 = f32[18,6,8,256]{3,2,1,0:T(8,128)S(1)} collective-permute-done((f32[18,6,8,256]{3,2,1,0:T(8,128)S(1)}, f32[18,6,8,256]{3,2,1,0:T(8,128)S(1)}, u32[]{:S(2)}, u32[]{:S(2)}) %collective-permute-start.7) | collective-permute-done | bytes 884768 | tf_op jit(solution)/shard_map/ppermute | solution.py:27
  117.3 1.9 fusion.29
  120.0 8.4 %collective-permute-done.8 = f32[6,8,8,256]{3,2,1,0:T(8,128)S(1)} collective-permute-done((f32[6,8,8,256]{3,2,1,0:T(8,128)S(1)}, f32[6,8,8,256]{3,2,1,0:T(8,128)S(1)}, u32[]{:S(2)}, u32[]{:S(2)}) %collective-permute-start.8) | collective-permute-done | bytes 393248 | tf_op jit(solution)/shard_map/ppermute | solution.py:29
  130.4 2.6 collective-permute-start.10
  133.3 19.8 %collective-permute-done.10 = f32[18,6,8,256]{3,2,1,0:T(8,128)S(1)} collective-permute-done((f32[18,6,8,256]{3,2,1,0:T(8,128)S(1)}, f32[18,6,8,256]{3,2,1,0:T(8,128)S(1)}, u32[]{:S(2)}, u32[]{:S(2)}) %collective-permute-start.10) | collective-permute-done | bytes 884768 | tf_op jit(solution)/shard_map/ppermute | solution.py:29
  153.1 20.1 %collective-permute-done.11 = f32[18,6,8,256]{3,2,1,0:T(8,128)S(1)} collective-permute-done((f32[18,6,8,256]{3,2,1,0:T(8,128)S(1)}, f32[18,6,8,256]{3,2,1,0:T(8,128)S(1)}, u32[]{:S(2)}, u32[]{:S(2)}) %collective-permute-start.11) | collective-permute-done | bytes 884768 | tf_op jit(solution)/shard_map/ppermute | solution.py:27
  173.7 1.9 fusion.38
  175.6 11.1 %all_gather.3 = f32[384,512]{1,0:T(8,128)S(1)} all-gather(f32[384,256]{1,0:T(8,128)S(1)} %bitcast.53), channel_id=1, replica_groups=mesh['dx'=4,'dy'=4,'band'=2] {'band'}, dimensions={1}, use_global_device_ids=true | all-gather | bytes 1179648 | tf_op jit(solution)/shard_map/all_gather | solution.py:65
  186.7 2.9 convolution_multiply_fusion
  190.8 92.1 %all-reduce.3.cloned.1.call-done = f32[512,512]{0,1:T(8,128)} async-done(((f32[512,512]{0,1:T(8,128)}), f32[512,512]{0,1:T(8,128)}) %all-reduce.3.cloned.1.call-update) | async-done | bytes 1048592 | tf_op jit(solution)/shard_map/psum | solution.py:76
  285.8 11.7 %cholesky.104 = f32[128,128]{1,0:T(8,128)S(1)} custom-call(f32[128,128]{1,0:T(8,128)S(1)} %cholesky.266), custom_call_target="Cholesky" | custom-call | tf_op jit(solution)/shard_map/jit(cholesky)/cholesky | solution.py:77
  297.6 9.8 %custom-call.31 = f32[1,128,128]{1,2,0:T(8,128)S(1)} custom-call(f32[1,128,128]{2,1,0:T(8,128)S(1)} %get-tuple-element.93), custom_call_target="InvertDiagBlocksLowerTriangular" | custom-call | tf_op jit(solution)/shard_map/jit(cholesky)/cholesky | solution.py:77
  310.0 11.9 %cholesky.217 = f32[128,128]{1,0:T(8,128)S(1)} custom-call(f32[128,128]{1,0:T(8,128)S(1)} %cholesky.270), custom_call_target="Cholesky" | custom-call | tf_op jit(solution)/shard_map/jit(cholesky)/cholesky | solution.py:77
  321.9 9.8 %custom-call.32 = f32[1,128,128]{1,2,0:T(8,128)S(1)} custom-call(f32[1,128,128]{2,1,0:T(8,128)S(1)} %get-tuple-element.90), custom_call_target="InvertDiagBlocksLowerTriangular" | custom-call | tf_op jit(solution)/shard_map/jit(cholesky)/cholesky | solution.py:77
  333.3 11.7 %cholesky.238 = f32[128,128]{1,0:T(8,128)S(1)} custom-call(f32[128,128]{1,0:T(8,128)S(1)} %cholesky.275), custom_call_target="Cholesky" | custom-call | tf_op jit(solution)/shard_map/jit(cholesky)/cholesky | solution.py:77
  345.7 9.8 %custom-call.33 = f32[1,128,128]{1,2,0:T(8,128)S(1)} custom-call(f32[1,128,128]{2,1,0:T(8,128)S(1)} %get-tuple-element.87), custom_call_target="InvertDiagBlocksLowerTriangular" | custom-call | tf_op jit(solution)/shard_map/jit(cholesky)/cholesky | solution.py:77
  356.9 11.9 %cholesky.255 = f32[128,128]{1,0:T(8,128)S(1)} custom-call(f32[128,128]{1,0:T(8,128)S(1)} %convolution_subtract_fusion.5), custom_call_target="Cholesky" | custom-call | tf_op jit(solution)/shard_map/jit(cholesky)/cholesky | solution.py:77
  373.9 14.1 %while.1 = (s32[]{:T(128)}, f32[512,512]{1,0:T(8,128)}, s32[4,2]{0,1:T(2,128)S(1)}, f32[4,128,128]{2,1,0:T(8,128)}, s32[]{:T(128)}) while((s32[]{:T(128)}, f32[512,512]{1,0:T(8,128)}, s32[4,2]{0,1:T(2,128)S(1)}, f32[4,128,128]{2,1,0:T(8,128)}, s32[]{:T(128)}) %tuple.58), condition=%wide.while_cond, body=%wide.while_body.sunk | while | flops 2 | bytes 132705 | solution.py:79
  374.5 2.9 bitcast_dynamic-update-slice_fusion.2
  378.1 2.9 bitcast_dynamic-update-slice_fusion.2
  381.6 2.9 bitcast_dynamic-update-slice_fusion.2
  385.1 2.8 bitcast_dynamic-update-slice_fusion.2
  387.9 40.1 %custom-call.34 = f32[4,128,128]{1,2,0:T(8,128)S(1)} custom-call(f32[4,128,128]{2,1,0:T(8,128)} %get-tuple-element.12), custom_call_target="InvertDiagBlocksLowerTriangular" | custom-call | tf_op jit(solution)/shard_map/jit(_solve_triangular)/triangular_solve | solution.py:79
  (96 shorter events, 38.1 us)
Async XLA Ops:
  6.5 9.9 %copy-start = (f32[6,8,8,256]{3,2,1,0:T(8,128)S(1)}, f32[6,8,8,256]{3,2,1,0:T(8,128)}, u32[]{:S(2)}) copy-start(f32[6,8,8,256]{3,2,1,0:T(8,128)} %param.2) | copy-start | bytes 1179652
  6.5 276.4 %all-reduce.3.cloned.1.call-start = ((), (), s32[]{:S(2)}) async-start(), calls=%async_computation | async-start | bytes 2097152 | tf_op jit(solution)/shard_map/psum | solution.py:76
  6.5 9.9 %collective-permute-start.1 = (f32[6,8,8,256]{3,2,1,0:T(8,128)}, f32[6,8,8,256]{3,2,1,0:T(8,128)S(1)}, u32[]{:S(2)}, u32[]{:S(2)}) collective-permute-start(f32[6,8,8,256]{3,2,1,0:T(8,128)} %param.2), channel_id=1, source_target_pairs={{0,8},{8,16},{16,24},{24,0},{1,9},{9,17},{17,25},{25,1},{2,10},{10... | collective-permute-start | bytes 1179656 | tf_op jit(solution)/shard_map/ppermute | solution.py:27
  7.0 11.8 %collective-permute-start = (f32[6,8,8,256]{3,2,1,0:T(8,128)}, f32[6,8,8,256]{3,2,1,0:T(8,128)S(1)}, u32[]{:S(2)}, u32[]{:S(2)}) collective-permute-start(f32[6,8,8,256]{3,2,1,0:T(8,128)} %param.2), channel_id=1, source_target_pairs={{8,0},{16,8},{24,16},{0,24},{9,1},{17,9},{25,17},{1,25},{10,2},{18... | collective-permute-start | bytes 1179656 | tf_op jit(solution)/shard_map/ppermute | solution.py:29
  18.9 3.9 copy-start.4
  19.1 23.7 %collective-permute-start.2 = (f32[18,6,8,256]{3,2,1,0:T(8,128)S(1)}, f32[18,6,8,256]{3,2,1,0:T(8,128)S(1)}, u32[]{:S(2)}, u32[]{:S(2)}) collective-permute-start(f32[18,6,8,256]{3,2,1,0:T(8,128)S(1)} %get-tuple-element.33), channel_id=1, source_target_pairs={{2,0},{4,2},{6,4},{0,6},{3,1},{5,3},{7,5},{1,7},{10,8},{12,10},{14... | collective-permute-start | bytes 2654216 | tf_op jit(solution)/shard_map/ppermute | solution.py:29
  22.7 39.6 %collective-permute-start.3 = (f32[18,6,8,256]{3,2,1,0:T(8,128)S(1)}, f32[18,6,8,256]{3,2,1,0:T(8,128)S(1)}, u32[]{:S(2)}, u32[]{:S(2)}) collective-permute-start(f32[18,6,8,256]{3,2,1,0:T(8,128)S(1)} %get-tuple-element.34), channel_id=1, source_target_pairs={{0,2},{2,4},{4,6},{6,0},{1,3},{3,5},{5,7},{7,1},{8,10},{10,12},{12... | collective-permute-start | bytes 2654216 | tf_op jit(solution)/shard_map/ppermute | solution.py:27
  64.3 9.9 %collective-permute-start.4 = (f32[6,8,8,256]{3,2,1,0:T(8,128)S(1)}, f32[6,8,8,256]{3,2,1,0:T(8,128)S(1)}, u32[]{:S(2)}, u32[]{:S(2)}) collective-permute-start(f32[6,8,8,256]{3,2,1,0:T(8,128)S(1)} %get-tuple-element.21), channel_id=1, source_target_pairs={{8,0},{16,8},{24,16},{0,24},{9,1},{17,9},{25,17},{1,25},{10,2},{18... | collective-permute-start | bytes 1179656 | tf_op jit(solution)/shard_map/ppermute | solution.py:29
  65.0 10.8 %collective-permute-start.5 = (f32[6,8,8,256]{3,2,1,0:T(8,128)S(1)}, f32[6,8,8,256]{3,2,1,0:T(8,128)S(1)}, u32[]{:S(2)}, u32[]{:S(2)}) collective-permute-start(f32[6,8,8,256]{3,2,1,0:T(8,128)S(1)} %get-tuple-element.21), channel_id=1, source_target_pairs={{0,8},{8,16},{16,24},{24,0},{1,9},{9,17},{17,25},{25,1},{2,10},{10... | collective-permute-start | bytes 1179656 | tf_op jit(solution)/shard_map/ppermute | solution.py:27
  76.1 21.8 %collective-permute-start.6 = (f32[18,6,8,256]{3,2,1,0:T(8,128)S(1)}, f32[18,6,8,256]{3,2,1,0:T(8,128)S(1)}, u32[]{:S(2)}, u32[]{:S(2)}) collective-permute-start(f32[18,6,8,256]{3,2,1,0:T(8,128)S(1)} %get-tuple-element.31), channel_id=1, source_target_pairs={{2,0},{4,2},{6,4},{0,6},{3,1},{5,3},{7,5},{1,7},{10,8},{12,10},{14... | collective-permute-start | bytes 2654216 | tf_op jit(solution)/shard_map/ppermute | solution.py:29
  77.9 38.8 %collective-permute-start.7 = (f32[18,6,8,256]{3,2,1,0:T(8,128)S(1)}, f32[18,6,8,256]{3,2,1,0:T(8,128)S(1)}, u32[]{:S(2)}, u32[]{:S(2)}) collective-permute-start(f32[18,6,8,256]{3,2,1,0:T(8,128)S(1)} %get-tuple-element.32), channel_id=1, source_target_pairs={{0,2},{2,4},{4,6},{6,0},{1,3},{3,5},{5,7},{7,1},{8,10},{10,12},{12... | collective-permute-start | bytes 2654216 | tf_op jit(solution)/shard_map/ppermute | solution.py:27
  119.2 9.2 %collective-permute-start.8 = (f32[6,8,8,256]{3,2,1,0:T(8,128)S(1)}, f32[6,8,8,256]{3,2,1,0:T(8,128)S(1)}, u32[]{:S(2)}, u32[]{:S(2)}) collective-permute-start(f32[6,8,8,256]{3,2,1,0:T(8,128)S(1)} %fusion.29), channel_id=1, source_target_pairs={{8,0},{16,8},{24,16},{0,24},{9,1},{17,9},{25,17},{1,25},{10,2},{18... | collective-permute-start | bytes 1179656 | tf_op jit(solution)/shard_map/ppermute | solution.py:29
  119.2 10.8 %collective-permute-start.9 = (f32[6,8,8,256]{3,2,1,0:T(8,128)S(1)}, f32[6,8,8,256]{3,2,1,0:T(8,128)S(1)}, u32[]{:S(2)}, u32[]{:S(2)}) collective-permute-start(f32[6,8,8,256]{3,2,1,0:T(8,128)S(1)} %fusion.29), channel_id=1, source_target_pairs={{0,8},{8,16},{16,24},{24,0},{1,9},{9,17},{17,25},{25,1},{2,10},{10... | collective-permute-start | bytes 1179656 | tf_op jit(solution)/shard_map/ppermute | solution.py:27
  130.4 22.7 %collective-permute-start.10 = (f32[18,6,8,256]{3,2,1,0:T(8,128)S(1)}, f32[18,6,8,256]{3,2,1,0:T(8,128)S(1)}, u32[]{:S(2)}, u32[]{:S(2)}) collective-permute-start(f32[18,6,8,256]{3,2,1,0:T(8,128)S(1)} %get-tuple-element.27), channel_id=1, source_target_pairs={{2,0},{4,2},{6,4},{0,6},{3,1},{5,3},{7,5},{1,7},{10,8},{12,10},{14... | collective-permute-start | bytes 2654216 | tf_op jit(solution)/shard_map/ppermute | solution.py:29
  133.0 40.2 %collective-permute-start.11 = (f32[18,6,8,256]{3,2,1,0:T(8,128)S(1)}, f32[18,6,8,256]{3,2,1,0:T(8,128)S(1)}, u32[]{:S(2)}, u32[]{:S(2)}) collective-permute-start(f32[18,6,8,256]{3,2,1,0:T(8,128)S(1)} %get-tuple-element.28), channel_id=1, source_target_pairs={{0,2},{2,4},{4,6},{6,0},{1,3},{3,5},{5,7},{7,1},{8,10},{10,12},{12... | collective-permute-start | bytes 2654216 | tf_op jit(solution)/shard_map/ppermute | solution.py:27
  282.9 1.7 copy-start.1
  284.8 1.0 copy-start.3
  345.0 83.4 %copy-start.2 = (f32[512,512]{1,0:T(8,128)S(1)}, f32[512,512]{1,0:T(8,128)}, u32[]{:S(2)}) copy-start(f32[512,512]{1,0:T(8,128)} %fusion.157) | copy-start | bytes 3145732
Sparse Core Ops, SparseCore 0:
  189.7 93.1 all-reduce.2
where the time goes:
time: 449 us; the launch traced here: 443 us
  waiting for transfers between devices  235 us (52%)
  other arithmetic  128 us (29%)
  local copies, waits for them, and re-layouts  23.5 us (5%)
  between operations  16.6 us (4%)
  matrix products  15.7 us (3%)
  starting transfers between devices  12 us (3%)
  blocking collectives  11.1 us (2%)
    psum x1, waiting for transfers between devices, shards(): correlation = lax.psum(partial_gram, ('dx', 'dy'))  92.1 us
    another operation x14, other arithmetic, shards(): factor = jnp.linalg.cholesky(correlation)  78.8 us
    ppermute x6, waiting for transfers between devices, with_halo(): lax.ppermute(head, axis, [((i + 1) % count, i) for i in range(count)])  78.7 us
    ppermute x6, waiting for transfers between devices, with_halo(): lax.ppermute(tail, axis, [(i, (i + 1) % count) for i in range(count)])  64.4 us
    another operation x3, other arithmetic, shards(): inverse = jax.scipy.linalg.solve_triangular(factor, eye, lower=True)  41.2 us
    another operation x12, local copies, waits for them, and re-layouts  14.1 us
    all_gather x1, blocking collectives, shards(): gathered = lax.all_gather(local, 'band', axis=1, tiled=True)  11.1 us
    ppermute x6, starting transfers between devices, with_halo(): lax.ppermute(head, axis, [((i + 1) % count, i) for i in range(count)])  10.8 us
  transfers between devices with their start and end apart: 13, of which 13 were waited for; matrix products, arithmetic and copies ran while one was open for 2% of the time, Pallas kernels for 0%

commit v1 on v0

--- a/solution.py
+++ b/solution.py
@@ -73,7 +73,8 @@
         )
         / total
     )
-    correlation = lax.psum(partial_gram, ("dx", "dy"))
+    pieces = lax.all_gather(partial_gram, ("dx", "dy"))
+    correlation = jnp.sum(pieces, axis=0)
     factor = jnp.linalg.cholesky(correlation)
     eye = jnp.eye(correlation.shape[0], dtype=jnp.float32)
     inverse = jax.scipy.linalg.solve_triangular(factor, eye, lower=True)

time: 449 us -> 488 us (1.087)
  waiting for transfers between devices: 235 us -> 268 us
  other arithmetic: 128 us -> 136 us
    all_gather x0 -> x1, waiting for transfers between devices: none -> 125 us  [shards(): pieces = lax.all_gather(partial_gram, ('dx', 'dy'))]
    psum x1 -> x0, waiting for transfers between devices: 92.1 us -> none  [shards(): correlation = lax.psum(partial_gram, ('dx', 'dy'))]
    reduce_sum x0 -> x1, other arithmetic: none -> 7.91 us  [shards(): correlation = jnp.sum(pieces, axis=0)]
  transfers between devices with their start and end apart: 13 -> 13, of which waited for: 13 -> 13; matrix products, arithmetic and copies ran while one was open for 2% -> 1% of each run, Pallas kernels for 0% -> 0%
where the time goes in v1:
time: 488 us; the launch traced here: 482 us
  waiting for transfers between devices  268 us (55%)
  other arithmetic  136 us (28%)
  local copies, waits for them, and re-layouts  22 us (5%)
  between operations  16.6 us (3%)
  matrix products  15.9 us (3%)
  starting transfers between devices  12 us (2%)
  blocking collectives  11.1 us (2%)
    all_gather x1, waiting for transfers between devices, shards(): pieces = lax.all_gather(partial_gram, ('dx', 'dy'))  125 us
    ppermute x6, waiting for transfers between devices, with_halo(): lax.ppermute(head, axis, [((i + 1) % count, i) for i in range(count)])  78.7 us
    another operation x14, other arithmetic, shards(): factor = jnp.linalg.cholesky(correlation)  78.6 us
    ppermute x6, waiting for transfers between devices, with_halo(): lax.ppermute(tail, axis, [(i, (i + 1) % count) for i in range(count)])  64.4 us
    another operation x3, other arithmetic, shards(): inverse = jax.scipy.linalg.solve_triangular(factor, eye, lower=True)  41.2 us
    another operation x12, local copies, waits for them, and re-layouts  13.9 us
    all_gather x1, blocking collectives, shards(): gathered = lax.all_gather(local, 'band', axis=1, tiled=True)  11.1 us
    ppermute x6, starting transfers between devices, with_halo(): lax.ppermute(head, axis, [((i + 1) % count, i) for i in range(count)])  10.8 us
  transfers between devices with their start and end apart: 13, of which 13 were waited for; matrix products, arithmetic and copies ran while one was open for 1% of the time, Pallas kernels for 0%

profile of v1, /device:TPU:0, one launch (start us, length us, event | category | flops | bytes accessed | tf_op | source)
XLA Modules:
  0.0 481.7 jit_solution(6598609146694521677)
XLA Ops:
  7.0 1.9 collective-permute-start
  13.8 2.6 collective-permute-done.1
  16.6 2.2 collective-permute-done
  19.1 3.7 collective-permute-start.2
  23.0 19.9 %collective-permute-done.2 = f32[18,6,8,256]{3,2,1,0:T(8,128)S(1)} collective-permute-done((f32[18,6,8,256]{3,2,1,0:T(8,128)S(1)}, f32[18,6,8,256]{3,2,1,0:T(8,128)S(1)}, u32[]{:S(2)}, u32[]{:S(2)}) %collective-permute-start.2) | collective-permute-done | bytes 884768 | tf_op jit(solution)/shard_map/ppermute | solution.py:29
  42.8 19.5 %collective-permute-done.3 = f32[18,6,8,256]{3,2,1,0:T(8,128)S(1)} collective-permute-done((f32[18,6,8,256]{3,2,1,0:T(8,128)S(1)}, f32[18,6,8,256]{3,2,1,0:T(8,128)S(1)}, u32[]{:S(2)}, u32[]{:S(2)}) %collective-permute-start.3) | collective-permute-done | bytes 884768 | tf_op jit(solution)/shard_map/ppermute | solution.py:27
  62.3 1.9 broadcast_multiply_fusion
  65.2 9.0 %collective-permute-done.4 = f32[6,8,8,256]{3,2,1,0:T(8,128)S(1)} collective-permute-done((f32[6,8,8,256]{3,2,1,0:T(8,128)S(1)}, f32[6,8,8,256]{3,2,1,0:T(8,128)S(1)}, u32[]{:S(2)}, u32[]{:S(2)}) %collective-permute-start.4) | collective-permute-done | bytes 393248 | tf_op jit(solution)/shard_map/ppermute | solution.py:29
  78.5 19.5 %collective-permute-done.6 = f32[18,6,8,256]{3,2,1,0:T(8,128)S(1)} collective-permute-done((f32[18,6,8,256]{3,2,1,0:T(8,128)S(1)}, f32[18,6,8,256]{3,2,1,0:T(8,128)S(1)}, u32[]{:S(2)}, u32[]{:S(2)}) %collective-permute-start.6) | collective-permute-done | bytes 884768 | tf_op jit(solution)/shard_map/ppermute | solution.py:29
  98.0 18.8 %collective-permute-done.7 = f32[18,6,8,256]{3,2,1,0:T(8,128)S(1)} collective-permute-done((f32[18,6,8,256]{3,2,1,0:T(8,128)S(1)}, f32[18,6,8,256]{3,2,1,0:T(8,128)S(1)}, u32[]{:S(2)}, u32[]{:S(2)}) %collective-permute-start.7) | collective-permute-done | bytes 884768 | tf_op jit(solution)/shard_map/ppermute | solution.py:27
  120.0 8.4 %collective-permute-done.8 = f32[6,8,8,256]{3,2,1,0:T(8,128)S(1)} collective-permute-done((f32[6,8,8,256]{3,2,1,0:T(8,128)S(1)}, f32[6,8,8,256]{3,2,1,0:T(8,128)S(1)}, u32[]{:S(2)}, u32[]{:S(2)}) %collective-permute-start.8) | collective-permute-done | bytes 393248 | tf_op jit(solution)/shard_map/ppermute | solution.py:29
  130.4 2.6 collective-permute-start.10
  133.3 19.8 %collective-permute-done.10 = f32[18,6,8,256]{3,2,1,0:T(8,128)S(1)} collective-permute-done((f32[18,6,8,256]{3,2,1,0:T(8,128)S(1)}, f32[18,6,8,256]{3,2,1,0:T(8,128)S(1)}, u32[]{:S(2)}, u32[]{:S(2)}) %collective-permute-start.10) | collective-permute-done | bytes 884768 | tf_op jit(solution)/shard_map/ppermute | solution.py:29
  153.1 20.1 %collective-permute-done.11 = f32[18,6,8,256]{3,2,1,0:T(8,128)S(1)} collective-permute-done((f32[18,6,8,256]{3,2,1,0:T(8,128)S(1)}, f32[18,6,8,256]{3,2,1,0:T(8,128)S(1)}, u32[]{:S(2)}, u32[]{:S(2)}) %collective-permute-start.11) | collective-permute-done | bytes 884768 | tf_op jit(solution)/shard_map/ppermute | solution.py:27
  173.7 1.9 fusion.38
  175.6 11.1 %all_gather.9 = f32[384,512]{1,0:T(8,128)S(1)} all-gather(f32[384,256]{1,0:T(8,128)S(1)} %bitcast.55), channel_id=1, replica_groups=mesh['dx'=4,'dy'=4,'band'=2] {'band'}, dimensions={1}, use_global_device_ids=true | all-gather | bytes 1179648 | tf_op jit(solution)/shard_map/all_gather | solution.py:65
  186.7 2.8 convolution_multiply_fusion
  190.8 124.8 %all-gather.3.cloned.1.call-done = f32[8192,512]{1,0:T(8,128)} async-done(((f32[512,512]{1,0:T(8,128)}), f32[8192,512]{1,0:T(8,128)}) %all-gather.3.cloned.1.call-update) | async-done | bytes 16777232 | tf_op jit(solution)/shard_map/all_gather | solution.py:76
  315.6 7.9 %reduce_sum.9 = f32[512,512]{1,0:T(8,128)S(1)} reduce(f32[16,512,512]{2,1,0:T(8,128)} %bitcast.54, f32[]{:T(128)} %constant.179.clone.1), dimensions={0}, to_apply=%region_0.1 | reduce | flops 3932160 | bytes 17825796 | tf_op jit(solution)/shard_map/reduce_sum | solution.py:77
  325.0 11.7 %cholesky.104 = f32[128,128]{1,0:T(8,128)S(1)} custom-call(f32[128,128]{1,0:T(8,128)S(1)} %cholesky.266), custom_call_target="Cholesky" | custom-call | tf_op jit(solution)/shard_map/jit(cholesky)/cholesky | solution.py:78
  336.9 9.8 %custom-call.31 = f32[1,128,128]{1,2,0:T(8,128)S(1)} custom-call(f32[1,128,128]{2,1,0:T(8,128)S(1)} %get-tuple-element.93), custom_call_target="InvertDiagBlocksLowerTriangular" | custom-call | tf_op jit(solution)/shard_map/jit(cholesky)/cholesky | solution.py:78
  349.3 11.9 %cholesky.217 = f32[128,128]{1,0:T(8,128)S(1)} custom-call(f32[128,128]{1,0:T(8,128)S(1)} %cholesky.270), custom_call_target="Cholesky" | custom-call | tf_op jit(solution)/shard_map/jit(cholesky)/cholesky | solution.py:78
  361.2 9.8 %custom-call.32 = f32[1,128,128]{1,2,0:T(8,128)S(1)} custom-call(f32[1,128,128]{2,1,0:T(8,128)S(1)} %get-tuple-element.90), custom_call_target="InvertDiagBlocksLowerTriangular" | custom-call | tf_op jit(solution)/shard_map/jit(cholesky)/cholesky | solution.py:78
  372.5 11.7 %cholesky.238 = f32[128,128]{1,0:T(8,128)S(1)} custom-call(f32[128,128]{1,0:T(8,128)S(1)} %cholesky.275), custom_call_target="Cholesky" | custom-call | tf_op jit(solution)/shard_map/jit(cholesky)/cholesky | solution.py:78
  384.9 9.8 %custom-call.33 = f32[1,128,128]{1,2,0:T(8,128)S(1)} custom-call(f32[1,128,128]{2,1,0:T(8,128)S(1)} %get-tuple-element.87), custom_call_target="InvertDiagBlocksLowerTriangular" | custom-call | tf_op jit(solution)/shard_map/jit(cholesky)/cholesky | solution.py:78
  396.4 11.7 %cholesky.255 = f32[128,128]{1,0:T(8,128)S(1)} custom-call(f32[128,128]{1,0:T(8,128)S(1)} %convolution_subtract_fusion.5), custom_call_target="Cholesky" | custom-call | tf_op jit(solution)/shard_map/jit(cholesky)/cholesky | solution.py:78
  413.1 13.9 %while.1 = (s32[]{:T(128)}, f32[512,512]{1,0:T(8,128)}, s32[4,2]{0,1:T(2,128)S(1)}, f32[4,128,128]{2,1,0:T(8,128)}, s32[]{:T(128)}) while((s32[]{:T(128)}, f32[512,512]{1,0:T(8,128)}, s32[4,2]{0,1:T(2,128)S(1)}, f32[4,128,128]{2,1,0:T(8,128)}, s32[]{:T(128)}) %tuple.58), condition=%wide.while_cond, body=%wide.while_body.sunk | while | flops 2 | bytes 132705 | solution.py:80
  413.8 2.8 bitcast_dynamic-update-slice_fusion.2
  417.3 2.8 bitcast_dynamic-update-slice_fusion.2
  420.7 2.8 bitcast_dynamic-update-slice_fusion.2
  424.2 2.8 bitcast_dynamic-update-slice_fusion.2
  427.0 40.1 %custom-call.34 = f32[4,128,128]{1,2,0:T(8,128)S(1)} custom-call(f32[4,128,128]{2,1,0:T(8,128)} %get-tuple-element.12), custom_call_target="InvertDiagBlocksLowerTriangular" | custom-call | tf_op jit(solution)/shard_map/jit(_solve_triangular)/triangular_solve | solution.py:80
  (95 shorter events, 39.0 us)
Async XLA Ops:
  6.5 9.9 %copy-start = (f32[6,8,8,256]{3,2,1,0:T(8,128)S(1)}, f32[6,8,8,256]{3,2,1,0:T(8,128)}, u32[]{:S(2)}) copy-start(f32[6,8,8,256]{3,2,1,0:T(8,128)} %param.2) | copy-start | bytes 1179652
  6.5 309.0 %all-gather.3.cloned.1.call-start = ((), (), s32[]{:S(2)}) async-start(), calls=%async_computation | async-start | bytes 17825792 | tf_op jit(solution)/shard_map/all_gather | solution.py:76
  6.5 9.9 %collective-permute-start.1 = (f32[6,8,8,256]{3,2,1,0:T(8,128)}, f32[6,8,8,256]{3,2,1,0:T(8,128)S(1)}, u32[]{:S(2)}, u32[]{:S(2)}) collective-permute-start(f32[6,8,8,256]{3,2,1,0:T(8,128)} %param.2), channel_id=1, source_target_pairs={{0,8},{8,16},{16,24},{24,0},{1,9},{9,17},{17,25},{25,1},{2,10},{10... | collective-permute-start | bytes 1179656 | tf_op jit(solution)/shard_map/ppermute | solution.py:27
  7.0 11.8 %collective-permute-start = (f32[6,8,8,256]{3,2,1,0:T(8,128)}, f32[6,8,8,256]{3,2,1,0:T(8,128)S(1)}, u32[]{:S(2)}, u32[]{:S(2)}) collective-permute-start(f32[6,8,8,256]{3,2,1,0:T(8,128)} %param.2), channel_id=1, source_target_pairs={{8,0},{16,8},{24,16},{0,24},{9,1},{17,9},{25,17},{1,25},{10,2},{18... | collective-permute-start | bytes 1179656 | tf_op jit(solution)/shard_map/ppermute | solution.py:29
  18.9 3.9 copy-start.3
  19.1 23.7 %collective-permute-start.2 = (f32[18,6,8,256]{3,2,1,0:T(8,128)S(1)}, f32[18,6,8,256]{3,2,1,0:T(8,128)S(1)}, u32[]{:S(2)}, u32[]{:S(2)}) collective-permute-start(f32[18,6,8,256]{3,2,1,0:T(8,128)S(1)} %get-tuple-element.33), channel_id=1, source_target_pairs={{2,0},{4,2},{6,4},{0,6},{3,1},{5,3},{7,5},{1,7},{10,8},{12,10},{14... | collective-permute-start | bytes 2654216 | tf_op jit(solution)/shard_map/ppermute | solution.py:29
  22.7 39.6 %collective-permute-start.3 = (f32[18,6,8,256]{3,2,1,0:T(8,128)S(1)}, f32[18,6,8,256]{3,2,1,0:T(8,128)S(1)}, u32[]{:S(2)}, u32[]{:S(2)}) collective-permute-start(f32[18,6,8,256]{3,2,1,0:T(8,128)S(1)} %get-tuple-element.34), channel_id=1, source_target_pairs={{0,2},{2,4},{4,6},{6,0},{1,3},{3,5},{5,7},{7,1},{8,10},{10,12},{12... | collective-permute-start | bytes 2654216 | tf_op jit(solution)/shard_map/ppermute | solution.py:27
  64.3 9.9 %collective-permute-start.4 = (f32[6,8,8,256]{3,2,1,0:T(8,128)S(1)}, f32[6,8,8,256]{3,2,1,0:T(8,128)S(1)}, u32[]{:S(2)}, u32[]{:S(2)}) collective-permute-start(f32[6,8,8,256]{3,2,1,0:T(8,128)S(1)} %get-tuple-element.21), channel_id=1, source_target_pairs={{8,0},{16,8},{24,16},{0,24},{9,1},{17,9},{25,17},{1,25},{10,2},{18... | collective-permute-start | bytes 1179656 | tf_op jit(solution)/shard_map/ppermute | solution.py:29
  65.0 10.8 %collective-permute-start.5 = (f32[6,8,8,256]{3,2,1,0:T(8,128)S(1)}, f32[6,8,8,256]{3,2,1,0:T(8,128)S(1)}, u32[]{:S(2)}, u32[]{:S(2)}) collective-permute-start(f32[6,8,8,256]{3,2,1,0:T(8,128)S(1)} %get-tuple-element.21), channel_id=1, source_target_pairs={{0,8},{8,16},{16,24},{24,0},{1,9},{9,17},{17,25},{25,1},{2,10},{10... | collective-permute-start | bytes 1179656 | tf_op jit(solution)/shard_map/ppermute | solution.py:27
  76.1 21.8 %collective-permute-start.6 = (f32[18,6,8,256]{3,2,1,0:T(8,128)S(1)}, f32[18,6,8,256]{3,2,1,0:T(8,128)S(1)}, u32[]{:S(2)}, u32[]{:S(2)}) collective-permute-start(f32[18,6,8,256]{3,2,1,0:T(8,128)S(1)} %get-tuple-element.31), channel_id=1, source_target_pairs={{2,0},{4,2},{6,4},{0,6},{3,1},{5,3},{7,5},{1,7},{10,8},{12,10},{14... | collective-permute-start | bytes 2654216 | tf_op jit(solution)/shard_map/ppermute | solution.py:29
  77.9 38.8 %collective-permute-start.7 = (f32[18,6,8,256]{3,2,1,0:T(8,128)S(1)}, f32[18,6,8,256]{3,2,1,0:T(8,128)S(1)}, u32[]{:S(2)}, u32[]{:S(2)}) collective-permute-start(f32[18,6,8,256]{3,2,1,0:T(8,128)S(1)} %get-tuple-element.32), channel_id=1, source_target_pairs={{0,2},{2,4},{4,6},{6,0},{1,3},{3,5},{5,7},{7,1},{8,10},{10,12},{12... | collective-permute-start | bytes 2654216 | tf_op jit(solution)/shard_map/ppermute | solution.py:27
  119.2 9.2 %collective-permute-start.8 = (f32[6,8,8,256]{3,2,1,0:T(8,128)S(1)}, f32[6,8,8,256]{3,2,1,0:T(8,128)S(1)}, u32[]{:S(2)}, u32[]{:S(2)}) collective-permute-start(f32[6,8,8,256]{3,2,1,0:T(8,128)S(1)} %fusion.29), channel_id=1, source_target_pairs={{8,0},{16,8},{24,16},{0,24},{9,1},{17,9},{25,17},{1,25},{10,2},{18... | collective-permute-start | bytes 1179656 | tf_op jit(solution)/shard_map/ppermute | solution.py:29
  119.2 10.8 %collective-permute-start.9 = (f32[6,8,8,256]{3,2,1,0:T(8,128)S(1)}, f32[6,8,8,256]{3,2,1,0:T(8,128)S(1)}, u32[]{:S(2)}, u32[]{:S(2)}) collective-permute-start(f32[6,8,8,256]{3,2,1,0:T(8,128)S(1)} %fusion.29), channel_id=1, source_target_pairs={{0,8},{8,16},{16,24},{24,0},{1,9},{9,17},{17,25},{25,1},{2,10},{10... | collective-permute-start | bytes 1179656 | tf_op jit(solution)/shard_map/ppermute | solution.py:27
  130.4 22.7 %collective-permute-start.10 = (f32[18,6,8,256]{3,2,1,0:T(8,128)S(1)}, f32[18,6,8,256]{3,2,1,0:T(8,128)S(1)}, u32[]{:S(2)}, u32[]{:S(2)}) collective-permute-start(f32[18,6,8,256]{3,2,1,0:T(8,128)S(1)} %get-tuple-element.27), channel_id=1, source_target_pairs={{2,0},{4,2},{6,4},{0,6},{3,1},{5,3},{7,5},{1,7},{10,8},{12,10},{14... | collective-permute-start | bytes 2654216 | tf_op jit(solution)/shard_map/ppermute | solution.py:29
  133.0 40.2 %collective-permute-start.11 = (f32[18,6,8,256]{3,2,1,0:T(8,128)S(1)}, f32[18,6,8,256]{3,2,1,0:T(8,128)S(1)}, u32[]{:S(2)}, u32[]{:S(2)}) collective-permute-start(f32[18,6,8,256]{3,2,1,0:T(8,128)S(1)} %get-tuple-element.28), channel_id=1, source_target_pairs={{0,2},{2,4},{4,6},{6,0},{1,3},{3,5},{5,7},{7,1},{8,10},{10,12},{12... | collective-permute-start | bytes 2654216 | tf_op jit(solution)/shard_map/ppermute | solution.py:27
  324.0 1.0 copy-start.2
  384.3 83.2 %copy-start.1 = (f32[512,512]{1,0:T(8,128)S(1)}, f32[512,512]{1,0:T(8,128)}, u32[]{:S(2)}) copy-start(f32[512,512]{1,0:T(8,128)} %fusion.157) | copy-start | bytes 3145732
Sparse Core Ops, SparseCore 0:
  189.7 125.8 all-gather.2
